TPU v7x, 256 devices: a whole 4x4x8 slice. The times are simulated.
256 devices in a mesh: seq: 64 (over y, z, core), tp: 4 (over x).
Axes of the slice: x: 4, y: 4, z: 8, core: 2. Of those that a mesh axis runs over, the one named last changes fastest.
Arguments:
- normed_input: bfloat16 [32768, 5376], P('seq', 'tp'), may hold values from -6 to 6
- query: bfloat16 [32768, 4096], P('seq', 'tp'), may hold values from -220 to 220, as said below
- key: bfloat16 [32768, 2048], P('seq', 'tp'), may hold values from -7 to 7
- value: bfloat16 [32768, 2048], P('seq', 'tp'), may hold values from -6 to 6
- adapter_down_maps: bfloat16 [64, 16, 5376], P(None, None, 'tp'), may hold values from -0.078125 to 0.078125
- adapter_up_maps: bfloat16 [64, 16, 2048], P(None, None, 'tp'), may hold values from -1.5 to 1.5
- block_adapter_choice: int32 [16], replicated, may hold values from 0 to 63
Outputs:
- attended: bfloat16 [32768, 4096], P('seq', 'tp')
Inputs may be any that keep to these rules, and one draw needn't show every extreme that they name: `query`: queries; some may be aligned with nearby keys.
All inputs are finite; a program needn't handle non-finite values.
Results may differ from a plain program's by a relative error of at most 0.014.
Values may be sent and summed in bfloat16 or wider, within the bound.
A program may use at most 128 MiB of HBM per device.

v0:
```python
import jax
import jax.numpy as jnp
from jax import lax
from jax.sharding import PartitionSpec as P

HEAD_WIDTH = 128
WINDOW = 1024
ADAPTER_RANK = 16
SEG_LEN = 2048


query_scale = 168.0 ** (-0.5)


def shifted(value, axis, steps):
    count = lax.axis_size(axis)
    leading, last = (max(0, -steps), min(count, count - steps))
    return lax.ppermute(value, axis, [(source, source + steps) for source in range(leading, last)])


def on_device(
    normed_input, query, key, value, adapter_down_maps, adapter_up_maps, block_adapter_choice
):
    tok = query.shape[0]
    columns = key.shape[1]
    kv_local = columns // HEAD_WIDTH
    q_local = query.shape[1] // HEAD_WIDTH
    group = q_local // kv_local
    where_seq = lax.axis_index("seq")
    blk = min(tok, SEG_LEN)
    nblk = tok // blk
    last_seg = block_adapter_choice.shape[0] - 1
    token_rows = where_seq * tok + jnp.arange(nblk, dtype=jnp.int32) * blk
    segment_adapter_ids = block_adapter_choice[jnp.clip(token_rows // SEG_LEN, 0, last_seg)]
    selected_down = adapter_down_maps[segment_adapter_ids]
    partial_value = jnp.einsum(
        "bsd,brd->bsr",
        normed_input.reshape(nblk, blk, -1),
        selected_down,
        preferred_element_type=jnp.float32,
    )
    rank_activation = lax.psum(partial_value.reshape(tok, ADAPTER_RANK).astype(jnp.bfloat16), "tp")
    hops = WINDOW // tok
    selected_up = adapter_up_maps[segment_adapter_ids]
    value_update = jnp.einsum(
        "bsr,brc->bsc",
        rank_activation.reshape(nblk, blk, ADAPTER_RANK),
        selected_up,
        preferred_element_type=jnp.float32,
    )
    value_full = (value + value_update.reshape(tok, columns)).astype(jnp.bfloat16)
    pieces = []
    current = (key, value_full)
    for step in range(hops):
        current = shifted((current[0], current[1]), "seq", 1)
        pieces.append((step + 1, current))
    received = pieces[::-1]
    rim_keys = [piece[1][0] for piece in received]
    rim_vals = [piece[1][1] for piece in received]
    keys_all = jnp.concatenate(rim_keys + [key], axis=0)
    vals_all = jnp.concatenate(rim_vals + [value_full], axis=0)
    qblock = min(512, tok)
    span = qblock + WINDOW
    start_global = where_seq * tok

    def one_block(index):
        first = index * qblock
        qrows = query.reshape(qblock, kv_local, group, HEAD_WIDTH)
        krows = keys_all.reshape(span, kv_local, HEAD_WIDTH)
        vrows = vals_all.reshape(span, kv_local, HEAD_WIDTH)
        scores = (
            jnp.einsum("qkgd,lkd->kgql", qrows, krows, preferred_element_type=jnp.float32)
            * query_scale
        )
        qpos = start_global + first + jnp.arange(qblock, dtype=jnp.int32)[:, None]
        kpos = start_global + first - WINDOW + jnp.arange(span, dtype=jnp.int32)[None, :]
        usable = (kpos <= qpos) & (qpos - kpos < WINDOW) & (kpos >= 0)
        scores = jnp.where(usable, scores, -1e30)
        top = jnp.max(scores, axis=-1, keepdims=True)
        expo = jnp.exp(scores - top)
        weights = (expo / jnp.sum(expo, axis=-1, keepdims=True)).astype(jnp.bfloat16)
        out = jnp.einsum("kgql,lkd->qkgd", weights, vrows, preferred_element_type=jnp.float32)
        return out.astype(jnp.bfloat16).reshape(qblock, q_local * HEAD_WIDTH)

    blocks = lax.map(one_block, jnp.arange(tok // qblock, dtype=jnp.int32))
    return blocks.reshape(tok, q_local * HEAD_WIDTH)


def solution(mesh):
    placed = (
        P("seq", "tp"),
        P("seq", "tp"),
        P("seq", "tp"),
        P("seq", "tp"),
        P(None, None, "tp"),
        P(None, None, "tp"),
        P(),
    )
    return jax.shard_map(
        on_device, mesh=mesh, in_specs=placed, out_specs=P("seq", "tp"), check_vma=False
    )
```

profile of v0, /device:TPU:24, one launch (start us, length us, event | category | flops | bytes accessed | tf_op | source)
XLA Modules:
  0.0 97.9 jit_solution(14657647938584223890)
XLA Ops:
  0.0 0.0 copy-start
  0.0 1.4 %dynamic-slice.8 = s32[1]{0:T(128)} dynamic-slice(s32[16]{0:T(128)} %param.13, s32[]{:T(128)} %bitcast.1), dynamic_slice_sizes={1} | dynamic-slice | bytes 12 | tf_op jit(solution)/shard_map/gather | solution.py:34
  3.1 0.0 copy-done
  3.1 1.6 %fusion.12 = bf16[512,16]{0,1:T(8,128)(2,1)S(1)} fusion(bf16[512,1344]{0,1:T(8,128)(2,1)} %param.7, bf16[64,16,1344]{2,1,0:T(8,128)(2,1)S(1)} %copy-done, s32[]{:T(128)} %bitcast.2), kind=kOutput, calls=%fused_computation.19 | convolution fusion | flops 22028288 | bytes 1437700 | tf_op jit(solution)/shard_map/bsd,brd->bsr/dot_general | solution.py:36
  4.7 16.9 %psum.7 = bf16[512,16]{0,1:T(8,128)(2,1)S(1)} all-reduce(bf16[512,16]{0,1:T(8,128)(2,1)S(1)} %fusion.12), channel_id=1, replica_groups=mesh['seq'=64,'tp'=4] {'tp'}, use_global_device_ids=true, to_apply=%region_0.1 | all-reduce | flops 8192 | bytes 32768 | tf_op jit(solution)/shard_map/psum | solution.py:42
  21.6 2.2 %fusion.11 = bf16[512,512]{1,0:T(8,128)(2,1)} fusion(bf16[512,16]{0,1:T(8,128)(2,1)S(1)} %psum.7, bf16[512,512]{1,0:T(8,128)(2,1)} %param.10, bf16[64,16,512]{2,1,0:T(8,128)(2,1)} %param.12, s32[]{:T(128)} %bitcast.2), kind=kOutput, calls=%fused_computation.17 | convolution fusion | flops 9175040 | bytes 1081856 | tf_op jit(solution)/shard_map/bsr,brc->bsc/dot_general | solution.py:45
  23.8 1.9 %collective-permute-start = (bf16[512,512]{1,0:T(8,128)(2,1)}, bf16[512,512]{1,0:T(8,128)(2,1)}, u32[]{:S(2)}, u32[]{:S(2)}) collective-permute-start(bf16[512,512]{1,0:T(8,128)(2,1)} %fusion.11), channel_id=1, source_target_pairs={{0,4},{4,8},{8,12},{12,16},{16,20},{20,24},{24,28},{28,32},{32,36}... | collective-permute-start | bytes 1572872 | tf_op jit(solution)/shard_map/ppermute | solution.py:18
  25.7 1.3 %copy.12 = bf16[512,512]{0,1:T(8,128)(2,1)S(1)} copy(bf16[512,512]{1,0:T(8,128)(2,1)} %param.9) | data formatting | bytes 1048576 | tf_op args[2]
  27.0 3.9 %collective-permute-start.2 = (bf16[512,512]{0,1:T(8,128)(2,1)S(1)}, bf16[512,512]{0,1:T(8,128)(2,1)}, u32[]{:S(2)}, u32[]{:S(2)}) collective-permute-start(bf16[512,512]{0,1:T(8,128)(2,1)S(1)} %copy.12), channel_id=1, source_target_pairs={{0,4},{4,8},{8,12},{12,16},{16,20},{20,24},{24,28},{28,32},{32,36}... | collective-permute-start | bytes 1572872 | tf_op jit(solution)/shard_map/ppermute | solution.py:18
  30.9 5.8 %collective-permute-done = bf16[512,512]{1,0:T(8,128)(2,1)} collective-permute-done((bf16[512,512]{1,0:T(8,128)(2,1)}, bf16[512,512]{1,0:T(8,128)(2,1)}, u32[]{:S(2)}, u32[]{:S(2)}) %collective-permute-start) | collective-permute-done | bytes 524320 | tf_op jit(solution)/shard_map/ppermute | solution.py:18
  36.7 1.9 %collective-permute-start.1 = (bf16[512,512]{1,0:T(8,128)(2,1)}, bf16[512,512]{1,0:T(8,128)(2,1)}, u32[]{:S(2)}, u32[]{:S(2)}) collective-permute-start(bf16[512,512]{1,0:T(8,128)(2,1)} %collective-permute-done), channel_id=1, source_target_pairs={{0,4},{4,8},{8,12},{12,16},{16,20},{20,24},{24,28},{28,32},{32,36}... | collective-permute-start | bytes 1572872 | tf_op jit(solution)/shard_map/ppermute | solution.py:18
  38.6 2.6 %reshape.60 = bf16[512,4,2,128]{3,2,1,0:T(2,128)(2,1)} reshape(bf16[512,1024]{1,0:T(8,128)(2,1)} %param.8) | data formatting | bytes 2097152 | tf_op jit(solution)/shard_map/while/body/eval_jaxpr/reshape | solution.py:68
  41.2 1.1 %collective-permute-done.2 = bf16[512,512]{0,1:T(8,128)(2,1)} collective-permute-done((bf16[512,512]{0,1:T(8,128)(2,1)S(1)}, bf16[512,512]{0,1:T(8,128)(2,1)}, u32[]{:S(2)}, u32[]{:S(2)}) %collective-permute-start.2) | collective-permute-done | bytes 524320 | tf_op jit(solution)/shard_map/ppermute | solution.py:18
  42.3 1.9 %collective-permute-start.3 = (bf16[512,512]{0,1:T(8,128)(2,1)}, bf16[512,512]{0,1:T(8,128)(2,1)}, u32[]{:S(2)}, u32[]{:S(2)}) collective-permute-start(bf16[512,512]{0,1:T(8,128)(2,1)} %collective-permute-done.2), channel_id=1, source_target_pairs={{0,4},{4,8},{8,12},{12,16},{16,20},{20,24},{24,28},{28,32},{32,36}... | collective-permute-start | bytes 1572872 | tf_op jit(solution)/shard_map/ppermute | solution.py:18
  44.3 1.9 %fusion.9 = pred[512,1536]{0,1:T(8,128)(4,1)} fusion(s32[512]{0:T(512)S(1)} %iota_add_fusion.1, s32[1536]{0:T(1024)S(1)} %iota_add_fusion, pred[1536]{0:T(1024)(128)(4,1)S(1)} %broadcast_compare_fusion), kind=kLoop, calls=%fused_computation.12 | loop fusion | flops 3932160 | bytes 796160 | tf_op jit(solution)/shard_map/while/body/eval_jaxpr/and | solution.py:77
  46.2 3.5 %collective-permute-done.1 = bf16[512,512]{1,0:T(8,128)(2,1)} collective-permute-done((bf16[512,512]{1,0:T(8,128)(2,1)}, bf16[512,512]{1,0:T(8,128)(2,1)}, u32[]{:S(2)}, u32[]{:S(2)}) %collective-permute-start.1) | collective-permute-done | bytes 524320 | tf_op jit(solution)/shard_map/ppermute | solution.py:18
  49.6 2.6 %pad_maximum_fusion = bf16[1536,512]{1,0:T(8,128)(2,1)} fusion(bf16[512,512]{1,0:T(8,128)(2,1)} %fusion.11, bf16[512,512]{1,0:T(8,128)(2,1)} %collective-permute-done, bf16[512,512]{1,0:T(8,128)(2,1)} %collective-permute-done.1), kind=kLoop, calls=%fused_computation.13 | loop fusion | flops 4718592 | bytes 3145728 | tf_op jit(solution)/shard_map/concatenate | solution.py:61
  52.2 2.6 %copy.22 = bf16[1536,512]{0,1:T(8,128)(2,1)} copy(bf16[1536,512]{1,0:T(8,128)(2,1)} %pad_maximum_fusion) | data formatting | bytes 3145728 | tf_op jit(solution)/shard_map/while/body/eval_jaxpr/reshape | solution.py:70
  54.9 0.0 copy-start.2
  54.9 0.4 collective-permute-done.3
  55.3 1.3 %pad_maximum_fusion.1 = bf16[1536,512]{0,1:T(8,128)(2,1)S(1)} fusion(bf16[512,512]{0,1:T(8,128)(2,1)S(1)} %copy.12, bf16[512,512]{0,1:T(8,128)(2,1)} %collective-permute-done.2, bf16[512,512]{0,1:T(8,128)(2,1)} %collective-permute-done.3), kind=kLoop, calls=%fused_computation.14 | loop fusion | flops 4718592 | bytes 3145728 | tf_op jit(solution)/shard_map/concatenate | solution.py:60
  56.6 0.0 copy-start.1
  56.6 1.1 %copy-done.1 = bf16[1536,512]{0,1:T(8,128)(2,1)} copy-done((bf16[1536,512]{0,1:T(8,128)(2,1)}, bf16[1536,512]{0,1:T(8,128)(2,1)S(1)}, u32[]{:S(2)}) %copy-start.1) | copy-done | bytes 1572888
  57.7 0.0 copy-done.2
  57.7 11.8 %fusion.15 = f32[4,1536,512,2]{2,1,3,0:T(8,128)} fusion(bf16[1536,4,128,1]{0,2,3,1:T(8,128)(2,1)S(1)} %bitcast.42, bf16[512,4,2,128]{3,2,1,0:T(2,128)(2,1)S(1)} %copy-done.2), kind=kOutput, calls=%fused_computation.21 | convolution fusion | flops 1610612736 | bytes 27787264 | tf_op jit(solution)/shard_map/while/body/eval_jaxpr/qkgd,lkd->kgql/dot_general | solution.py:72
  69.5 10.9 %fusion.30 = f32[4,2,512]{2,1,0:T(2,128)S(1)} fusion(pred[512,1536]{0,1:T(8,128)(4,1)} %fusion.9, bf16[1536,4,128,1]{0,2,3,1:T(8,128)(2,1)} %bitcast.43, bf16[512,4,2,128]{3,2,1,0:T(2,128)(2,1)} %reshape.60), kind=kOutput, calls=%fused_computation.37 | convolution fusion | flops 1635780096 | bytes 3424256 | tf_op jit(solution)/shard_map/while/body/eval_jaxpr/sub | solution.py:80
  80.4 15.2 %fusion.10 = bf16[4,128,2,512]{3,1,2,0:T(8,128)(2,1)} fusion(bf16[1536,4,128,1]{0,2,3,1:T(8,128)(2,1)} %bitcast.44, f32[4,2,512]{2,1,0:T(2,128)S(1)} %fusion.30, f32[4,1536,512,2]{2,1,3,0:T(8,128)} %fusion.15, pred[512,1536]{0,1:T(8,128)(4,1)} %fusion.9), kind=kOutput, calls=%fused_computation.15 | convolution fusion | flops 1642599936 | bytes 28590080 | tf_op jit(solution)/shard_map/while/body/eval_jaxpr/kgql,lkd->qkgd/dot_general | solution.py:82
  95.6 2.3 %copy.18 = bf16[512,1024]{1,0:T(8,128)(2,1)} copy(bf16[512,1024]{0,1:T(8,128)(2,1)} %bitcast.45) | data formatting | bytes 2097152 | tf_op jit(solution)/shard_map/reshape | solution.py:86
  (3 shorter events, 0.0 us)
Async XLA Ops:
  0.0 3.1 %copy-start = (bf16[64,16,1344]{2,1,0:T(8,128)(2,1)S(1)}, bf16[64,16,1344]{2,1,0:T(8,128)(2,1)}, u32[]{:S(2)}) copy-start(bf16[64,16,1344]{2,1,0:T(8,128)(2,1)} %param.11) | copy-start | bytes 8257540
  23.8 12.9 %collective-permute-start = (bf16[512,512]{1,0:T(8,128)(2,1)}, bf16[512,512]{1,0:T(8,128)(2,1)}, u32[]{:S(2)}, u32[]{:S(2)}) collective-permute-start(bf16[512,512]{1,0:T(8,128)(2,1)} %fusion.11), channel_id=1, source_target_pairs={{0,4},{4,8},{8,12},{12,16},{16,20},{20,24},{24,28},{28,32},{32,36}... | collective-permute-start | bytes 1572872 | tf_op jit(solution)/shard_map/ppermute | solution.py:18
  27.0 15.4 %collective-permute-start.2 = (bf16[512,512]{0,1:T(8,128)(2,1)S(1)}, bf16[512,512]{0,1:T(8,128)(2,1)}, u32[]{:S(2)}, u32[]{:S(2)}) collective-permute-start(bf16[512,512]{0,1:T(8,128)(2,1)S(1)} %copy.12), channel_id=1, source_target_pairs={{0,4},{4,8},{8,12},{12,16},{16,20},{20,24},{24,28},{28,32},{32,36}... | collective-permute-start | bytes 1572872 | tf_op jit(solution)/shard_map/ppermute | solution.py:18
  36.7 12.9 %collective-permute-start.1 = (bf16[512,512]{1,0:T(8,128)(2,1)}, bf16[512,512]{1,0:T(8,128)(2,1)}, u32[]{:S(2)}, u32[]{:S(2)}) collective-permute-start(bf16[512,512]{1,0:T(8,128)(2,1)} %collective-permute-done), channel_id=1, source_target_pairs={{0,4},{4,8},{8,12},{12,16},{16,20},{20,24},{24,28},{28,32},{32,36}... | collective-permute-start | bytes 1572872 | tf_op jit(solution)/shard_map/ppermute | solution.py:18
  42.3 12.9 %collective-permute-start.3 = (bf16[512,512]{0,1:T(8,128)(2,1)}, bf16[512,512]{0,1:T(8,128)(2,1)}, u32[]{:S(2)}, u32[]{:S(2)}) collective-permute-start(bf16[512,512]{0,1:T(8,128)(2,1)} %collective-permute-done.2), channel_id=1, source_target_pairs={{0,4},{4,8},{8,12},{12,16},{16,20},{20,24},{24,28},{28,32},{32,36}... | collective-permute-start | bytes 1572872 | tf_op jit(solution)/shard_map/ppermute | solution.py:18
  54.9 2.8 %copy-start.2 = (bf16[512,4,2,128]{3,2,1,0:T(2,128)(2,1)S(1)}, bf16[512,4,2,128]{3,2,1,0:T(2,128)(2,1)}, u32[]{:S(2)}) copy-start(bf16[512,4,2,128]{3,2,1,0:T(2,128)(2,1)} %reshape.60) | copy-start | bytes 3145732
  56.6 1.1 %copy-start.1 = (bf16[1536,512]{0,1:T(8,128)(2,1)}, bf16[1536,512]{0,1:T(8,128)(2,1)S(1)}, u32[]{:S(2)}) copy-start(bf16[1536,512]{0,1:T(8,128)(2,1)S(1)} %pad_maximum_fusion.1) | copy-start | bytes 4718596
where the time goes:
time: 98.3 us; the launch traced here: 97.9 us
  matrix products  41.7 us (42%)
  blocking collectives  16.9 us (17%)
  local copies, waits for them, and re-layouts  11.3 us (11%)
  waiting for transfers between devices  10.7 us (11%)
  starting transfers between devices  9.66 us (10%)
  other arithmetic  5.86 us (6%)
  between operations  1.78 us (2%)
    psum x1, blocking collectives, on_device(): lax.psum(partial_value.reshape(tok, ADAPTER_RANK).astype(jnp.bfloat16), '...  16.9 us
    dot_general x1, matrix products, one_block(): jnp.einsum('kgql,lkd->qkgd', weights, vrows, preferred_element_type=jnp.f...  15.2 us
    dot_general x1, matrix products, one_block(): jnp.einsum('qkgd,lkd->kgql', qrows, krows, preferred_element_type=jnp.flo...  11.8 us
    sub x1, matrix products, one_block(): expo = jnp.exp(scores - top)  10.9 us
    ppermute x4, waiting for transfers between devices, shifted(): lax.ppermute(value, axis, [(source, source + steps) for source in range(l...  10.7 us
    ppermute x4, starting transfers between devices, shifted(): lax.ppermute(value, axis, [(source, source + steps) for source in range(l...  9.66 us
    reshape x1, local copies, waits for them, and re-layouts, one_block(): vrows = vals_all.reshape(span, kv_local, HEAD_WIDTH)  2.64 us
    concatenate x1, other arithmetic, on_device(): vals_all = jnp.concatenate(rim_vals + [value_full], axis=0)  2.61 us
  transfers between devices with their start and end apart: 4, of which 4 were waited for; matrix products, arithmetic and copies ran while one was open for 11% of the time, Pallas kernels for 0%

commit v1 on v0

v1 whole, which is shorter than its diff:
```python
import functools

import jax
import jax.numpy as jnp
from jax import lax
from jax.experimental import pallas as pl
from jax.experimental.pallas import tpu as pltpu
from jax.sharding import PartitionSpec as P

HEAD_WIDTH = 128
SEG_LEN = 2048
MESH = pl.DeviceIdType.MESH
EARLY = 3
SCALE2 = 168.0 ** (-0.5) * 1.4426950408889634
NEG = -1e30
BIG = 1e30


def kernel(
    n_seq, n_tp,
    choice_ref, x_ref, q_ref, k_ref, v_ref, down_ref, up_ref,
    out_ref,
    x_v, down_v, up_v, q_v, kall, vraw, vf, lat, latall, upsel, out_v,
    in_sem, kv_sem, out_sem,
    ring_send, ring_recv, pair_send, pair_recv,
    part_send, part_recv, lat_send, lat_recv,
):
    me = lax.axis_index("seq")
    tp = lax.axis_index("tp")
    core = lax.rem(me, 2)
    tok = q_ref.shape[0]
    kv = k_ref.shape[1] // HEAD_WIDTH
    half = tok // 2
    span = 2 * tok + half

    def seq_at(step):
        return lax.rem(me + n_seq + step, n_seq)

    barrier = pltpu.get_barrier_semaphore()
    for step in (1, 2, -1, -2):
        pl.semaphore_signal(barrier, inc=1, device_id=(seq_at(step), tp), device_id_type=MESH)
    for step in range(1, n_tp):
        pl.semaphore_signal(
            barrier, inc=1, device_id=(me, lax.rem(tp + step, n_tp)), device_id_type=MESH
        )

    loads = [
        pltpu.make_async_copy(x_ref, x_v, in_sem.at[0]),
        pltpu.make_async_copy(down_ref, down_v, in_sem.at[1]),
        pltpu.make_async_copy(up_ref, up_v, in_sem.at[2]),
        pltpu.make_async_copy(q_ref, q_v, in_sem.at[3]),
    ]
    for load in loads:
        load.start()

    def columns(head):
        return pl.ds(pl.multiple_of(head * HEAD_WIDTH, HEAD_WIDTH), HEAD_WIDTH)

    def own_copy(which, head):
        src = (k_ref, v_ref)[which].at[:, columns(head)]
        dst = (kall, vraw)[which].at[head, pl.ds(2 * tok, tok), :]
        return pltpu.make_async_copy(src, dst, kv_sem.at[which, head])

    for head in range(kv):
        own_copy(0, head).start()
        own_copy(1, head).start()

    def ring_copy(which, head):
        return pltpu.make_async_remote_copy(
            src_ref=(k_ref, v_ref)[which].at[:, columns(head)],
            dst_ref=(kall, vraw)[which].at[head, pl.ds(0, tok), :],
            send_sem=ring_send.at[which, head],
            recv_sem=ring_recv.at[which, head],
            device_id=(seq_at(2), tp),
            device_id_type=MESH,
        )

    def give_copy(which, head):
        return pltpu.make_async_remote_copy(
            src_ref=(k_ref, v_ref)[which].at[:, columns(head)],
            dst_ref=(kall, vraw)[which].at[head, pl.ds(tok, tok), :],
            send_sem=pair_send.at[which, head],
            recv_sem=pair_recv.at[which, head],
            device_id=(seq_at(1), tp),
            device_id_type=MESH,
        )

    def relay_copy(which, head):
        buffer = (kall, vraw)[which]
        return pltpu.make_async_remote_copy(
            src_ref=buffer.at[head, pl.ds(0, tok), :],
            dst_ref=buffer.at[head, pl.ds(tok, tok), :],
            send_sem=pair_send.at[which, head],
            recv_sem=pair_recv.at[which, head],
            device_id=(seq_at(-1), tp),
            device_id_type=MESH,
        )

    pl.semaphore_wait(barrier, 4 + n_tp - 1)

    order = [(which, head) for head in range(kv) for which in range(2)]
    for which, head in order[:EARLY]:
        ring_copy(which, head).start()

    @pl.when(core == 0)
    def _():
        for which, head in order:
            give_copy(which, head).start()

    loads[0].wait()
    loads[1].wait()
    chip_seg = (me * tok) // SEG_LEN
    lat[tp] = jnp.dot(
        down_v[choice_ref[chip_seg]], x_v[...], preferred_element_type=jnp.float32
    )

    def part_copy(step):
        return pltpu.make_async_remote_copy(
            src_ref=lat.at[tp],
            dst_ref=lat.at[tp],
            send_sem=part_send.at[step - 1],
            recv_sem=part_recv.at[step - 1],
            device_id=(me, lax.rem(tp + step, n_tp)),
            device_id_type=MESH,
        )

    def part_arrival(step):
        slot = lat.at[lax.rem(tp + n_tp - step, n_tp)]
        return pltpu.make_async_remote_copy(
            src_ref=slot,
            dst_ref=slot,
            send_sem=part_send.at[step - 1],
            recv_sem=part_recv.at[step - 1],
            device_id=(me, lax.rem(tp + step, n_tp)),
            device_id_type=MESH,
        )

    for step in range(1, n_tp):
        part_copy(step).start()

    loads[2].wait()
    for source in range(3):
        segment = (seq_at(source - 2) * tok) // SEG_LEN
        upsel[source] = up_v[choice_ref[segment]]

    for step in range(1, n_tp):
        part_arrival(step).wait_recv()
    total = lat[0]
    for step in range(1, n_tp):
        total = total + lat[step]
    latall[2] = total.astype(jnp.bfloat16)

    def lat_copy(step):
        return pltpu.make_async_remote_copy(
            src_ref=latall.at[2],
            dst_ref=latall.at[2 - step],
            send_sem=lat_send.at[step - 1],
            recv_sem=lat_recv.at[step - 1],
            device_id=(seq_at(step), tp),
            device_id_type=MESH,
        )

    lat_copy(1).start()
    lat_copy(2).start()
    for which, head in order[EARLY:]:
        ring_copy(which, head).start()

    loads[3].wait()
    lat_copy(1).wait_recv()
    lat_copy(2).wait_recv()

    row = lax.broadcasted_iota(jnp.int32, (half, half), 0)
    col = lax.broadcasted_iota(jnp.int32, (half, half), 1)
    later = col > row
    have = [me >= 2, me >= 1, None]

    def one_head(head, carry):
        own_copy(0, head).wait()
        own_copy(1, head).wait()
        ring_copy(0, head).wait_recv()
        ring_copy(1, head).wait_recv()

        @pl.when(core == 1)
        def _():
            relay_copy(0, head).start()
            relay_copy(1, head).start()

        give_copy(0, head).wait_recv()
        give_copy(1, head).wait_recv()
        for source in range(3):
            rows = pl.ds(source * tok, tok)
            update = lax.dot_general(
                latall[source], upsel[source, :, columns(head)],
                (((0,), (0,)), ((), ())), preferred_element_type=jnp.float32,
            )
            vf[rows, :] = (vraw[head, rows, :].astype(jnp.float32) + update).astype(jnp.bfloat16)

        for block in range(2):
            first = block * half
            keys = kall[head, pl.ds(first, span), :]
            vals = vf[pl.ds(first, span), :]
            edges = [0, 2 * half - first, 4 * half - first, span]
            for member in range(2):
                at = pl.multiple_of((head * 2 + member) * HEAD_WIDTH, HEAD_WIDTH)
                rows = q_v[pl.ds(first, half), pl.ds(at, HEAD_WIDTH)]
                scores = lax.dot_general(
                    rows, keys, (((1,), (1,)), ((), ())), preferred_element_type=jnp.float32
                )
                scores = jnp.concatenate(
                    [
                        jnp.where(later, scores[:, :half], NEG),
                        scores[:, half : span - half],
                        jnp.where(later, NEG, scores[:, span - half :]),
                    ],
                    axis=1,
                )
                top = None
                for source in range(3):
                    part = jnp.max(scores[:, edges[source] : edges[source + 1]], axis=1, keepdims=True)
                    if have[source] is not None:
                        part = jnp.where(have[source], part, NEG)
                    top = part if top is None else jnp.maximum(top, part)
                top = top * SCALE2
                expo = []
                for source in range(3):
                    shift = top if have[source] is None else jnp.where(have[source], top, BIG)
                    expo.append(
                        jnp.exp2(scores[:, edges[source] : edges[source + 1]] * SCALE2 - shift)
                    )
                expo = jnp.concatenate(expo, axis=1)
                norm = jnp.sum(expo, axis=1, keepdims=True)
                out = jnp.dot(expo.astype(jnp.bfloat16), vals, preferred_element_type=jnp.float32)
                out_v[pl.ds(first, half), pl.ds(at, HEAD_WIDTH)] = (out / norm).astype(jnp.bfloat16)
        out_copy(head).start()
        return carry

    def out_copy(head):
        at = pl.ds(pl.multiple_of(head * 2 * HEAD_WIDTH, 2 * HEAD_WIDTH), 2 * HEAD_WIDTH)
        return pltpu.make_async_copy(out_v.at[:, at], out_ref.at[:, at], out_sem.at[head])

    lax.fori_loop(0, kv, one_head, 0)

    for step in range(1, n_tp):
        part_copy(step).wait_send()
    lat_copy(1).wait_send()
    lat_copy(2).wait_send()
    for which, head in order:
        ring_copy(which, head).wait_send()
        give_copy(which, head).wait_send()
    for head in range(kv):
        out_copy(head).wait()


def on_device(
    n_seq, n_tp,
    normed_input, query, key, value, adapter_down_maps, adapter_up_maps, block_adapter_choice,
):
    tok, width = normed_input.shape
    kv = key.shape[1] // HEAD_WIDTH
    count, rank, columns = adapter_up_maps.shape
    bf16 = jnp.bfloat16
    dma = pltpu.SemaphoreType.DMA
    hbm = pl.BlockSpec(memory_space=pl.ANY)
    return pl.pallas_call(
        functools.partial(kernel, n_seq, n_tp),
        out_shape=jax.ShapeDtypeStruct(query.shape, bf16),
        in_specs=[pl.BlockSpec(memory_space=pltpu.SMEM)] + [hbm] * 6,
        out_specs=hbm,
        scratch_shapes=[
            pltpu.VMEM((width, tok), bf16),
            pltpu.VMEM((count, rank, width), bf16),
            pltpu.VMEM((count, rank, columns), bf16),
            pltpu.VMEM(query.shape, bf16),
            pltpu.VMEM((kv, 3 * tok, HEAD_WIDTH), bf16),
            pltpu.VMEM((kv, 3 * tok, HEAD_WIDTH), bf16),
            pltpu.VMEM((3 * tok, HEAD_WIDTH), bf16),
            pltpu.VMEM((n_tp, rank, tok), jnp.float32),
            pltpu.VMEM((3, rank, tok), bf16),
            pltpu.VMEM((3, rank, columns), bf16),
            pltpu.VMEM(query.shape, bf16),
            dma((4,)),
            dma((2, kv)),
            dma((kv,)),
            dma((2, kv)), dma((2, kv)), dma((2, kv)), dma((2, kv)),
            dma((n_tp - 1,)), dma((n_tp - 1,)), dma((2,)), dma((2,)),
        ],
        compiler_params=pltpu.CompilerParams(collective_id=0, has_side_effects=True),
    )(
        block_adapter_choice, normed_input.T, query, key, value,
        adapter_down_maps, adapter_up_maps,
    )


def solution(mesh):
    placed = (
        P("seq", "tp"),
        P("seq", "tp"),
        P("seq", "tp"),
        P("seq", "tp"),
        P(None, None, "tp"),
        P(None, None, "tp"),
        P(),
    )
    return jax.shard_map(
        functools.partial(on_device, mesh.shape["seq"], mesh.shape["tp"]),
        mesh=mesh, in_specs=placed, out_specs=P("seq", "tp"), check_vma=False,
    )
```

time: 98.3 us -> 42.2 us (0.43)
  the two profiles are of different devices: /device:TPU:24 before, /device:TPU:1 now
where the time goes in v1:
time: 42.2 us; the launch traced here: 42.1 us
  Pallas kernels  39.8 us (94%)
  local copies, waits for them, and re-layouts  2.26 us (5%)
    pallas_call x1, Pallas kernels, on_device(): pl.pallas_call(functools.partial(kernel, n_seq, n_tp), out_shape=jax.Shap...  39.8 us
    unnamed x1, local copies, waits for them, and re-layouts  2.26 us

profile of v1, /device:TPU:1, one launch (start us, length us, event | category | flops | bytes accessed | tf_op | source)
XLA Modules:
  0.0 42.1 jit_solution(8488148463593455892)
XLA Ops:
  0.0 39.8 %shard_map.73 = bf16[512,1024]{1,0:T(8,128)(2,1)} custom-call(s32[16]{0:T(128)} %choice_ref.1, bf16[1344,512]{1,0:T(8,128)(2,1)} %bitcast.1, bf16[512,1024]{1,0:T(8,128)(2,1)} %q_ref.1, bf16[512,512]{1,0:T(8,128)(2,1)} %k_ref.1, bf16[512,512]{1,0:T(8,128)(2,1)} %v_ref.1, bf16[64,16,1344]{2,1,0:T(8,128)(2,1)} %down_ref.1, bf16[64,16,512]{2,1,0:T(8,128)(2,1)} %up_ref.1), custom_call_target="tpu_custom_call" | custom-call | tf_op jit(solution)/shard_map/pallas_call | solution.py:264
  39.8 2.3 %copy.9 = bf16[512,1024]{1,0:T(8,128)(2,1)} copy(bf16[512,1024]{1,0:T(8,128)(2,1)} %shard_map.73) | data formatting | bytes 2097152

commit v2 on v1

v2 whole, which is shorter than its diff:
```python
import functools

import jax
import jax.numpy as jnp
from jax import lax
from jax.experimental import pallas as pl
from jax.experimental.pallas import tpu as pltpu
from jax.sharding import PartitionSpec as P

HEAD_WIDTH = 128
SEG_LEN = 2048
MESH = pl.DeviceIdType.MESH
EARLY = 6
SCALE2 = 168.0 ** (-0.5) * 1.4426950408889634
NEG = -1e30
BIG = 1e30
ROW = 16
DETOUR = ((1, 1, 0), (1, 2, 0), (1, 3, 0))


def kernel(
    n_seq, n_tp,
    choice_ref, x_ref, q_ref, k_ref, v_ref, down_ref, up_ref,
    out_ref,
    x_v, down_v, up_v, q_v, kall, vraw, vf, lat, latall, upsel, hold, m_s, l_s, acc_s,
    in_sem, kv_sem,
    ring_send, ring_recv, pair_send, pair_recv,
    part_send, part_recv, lat_send, lat_recv,
    hop_send, hop_recv, fwd_send,
):
    me = lax.axis_index("seq")
    tp = lax.axis_index("tp")
    core = lax.rem(me, 2)
    partner = me + 1 - 2 * core
    place = lax.rem(me, ROW)
    last_row = n_seq - ROW
    n_flow = n_seq // ROW - 1
    tok = q_ref.shape[0]
    kv = k_ref.shape[1] // HEAD_WIDTH
    half = tok // 2
    span = 2 * tok + half
    has_prev = me >= 2
    has_pair = me >= 1
    has_next = me < n_seq - 2
    turns = jnp.logical_and(place >= ROW - 2, has_next)
    lands = jnp.logical_and(place < 2, has_prev)
    relays = jnp.logical_not(has_next)

    def tp_at(step):
        return lax.rem(tp + n_tp + step, n_tp)

    @pl.when(jnp.logical_not(has_prev))
    def _():
        for buffer in (kall, vraw):
            buffer[:, : 2 * tok, :] = jnp.zeros((kv, 2 * tok, HEAD_WIDTH), buffer.dtype)
        latall[...] = jnp.zeros_like(latall)

    barrier = pltpu.get_barrier_semaphore()

    def greet(device):
        pl.semaphore_signal(barrier, inc=1, device_id=device, device_id_type=MESH)

    greet((partner, tp))

    @pl.when(has_prev)
    def _():
        greet((me - 2, tp))

    @pl.when(jnp.logical_and(has_prev, core == 0))
    def _():
        greet((me - 1, tp))

    for step in range(1, n_tp):
        greet((me, tp_at(step)))

    if DETOUR:
        @pl.when(lands)
        def _():
            greet((n_seq - 2 + core, tp))

        @pl.when(relays)
        def _():
            for flow in range(n_flow):
                greet((flow * ROW + place, tp))

    loads = [
        pltpu.make_async_copy(x_ref, x_v, in_sem.at[0]),
        pltpu.make_async_copy(down_ref, down_v, in_sem.at[1]),
        pltpu.make_async_copy(up_ref, up_v, in_sem.at[2]),
        pltpu.make_async_copy(q_ref, q_v, in_sem.at[3]),
    ]
    loads[0].start()
    loads[1].start()

    def columns(head):
        return pl.ds(pl.multiple_of(head * HEAD_WIDTH, HEAD_WIDTH), HEAD_WIDTH)

    def own_copy(which, head):
        src = (k_ref, v_ref)[which].at[:, columns(head)]
        dst = (kall, vraw)[which].at[head, pl.ds(2 * tok, tok), :]
        return pltpu.make_async_copy(src, dst, kv_sem.at[which, head])

    def ring_copy(which, head, part):
        rows = pl.ds(part * half, half)
        return pltpu.make_async_remote_copy(
            src_ref=(k_ref, v_ref)[which].at[rows, columns(head)],
            dst_ref=(kall, vraw)[which].at[head, rows, :],
            send_sem=ring_send.at[which, head, part],
            recv_sem=ring_recv.at[which, head, part],
            device_id=(me + 2, tp),
            device_id_type=MESH,
        )

    def give_copy(which, head, part):
        rows = pl.ds(part * half, half)
        return pltpu.make_async_remote_copy(
            src_ref=(k_ref, v_ref)[which].at[rows, columns(head)],
            dst_ref=(kall, vraw)[which].at[head, pl.ds(tok + part * half, half), :],
            send_sem=pair_send.at[which, head, part],
            recv_sem=pair_recv.at[which, head, part],
            device_id=(partner, tp),
            device_id_type=MESH,
        )

    def relay_copy(which, head, part):
        buffer = (kall, vraw)[which]
        return pltpu.make_async_remote_copy(
            src_ref=buffer.at[head, pl.ds(part * half, half), :],
            dst_ref=buffer.at[head, pl.ds(tok + part * half, half), :],
            send_sem=pair_send.at[which, head, part],
            recv_sem=pair_recv.at[which, head, part],
            device_id=(partner, tp),
            device_id_type=MESH,
        )

    def hop_copy(flow, index):
        which, head, part = DETOUR[index]
        return pltpu.make_async_remote_copy(
            src_ref=(k_ref, v_ref)[which].at[pl.ds(part * half, half), columns(head)],
            dst_ref=hold.at[flow, index],
            send_sem=hop_send.at[index],
            recv_sem=hop_recv.at[flow, index],
            device_id=(last_row + place, tp),
            device_id_type=MESH,
        )

    def forward_copy(flow, index):
        which, head, part = DETOUR[index]
        return pltpu.make_async_remote_copy(
            src_ref=hold.at[flow, index],
            dst_ref=(kall, vraw)[which].at[head, pl.ds(part * half, half), :],
            send_sem=fwd_send.at[flow, index],
            recv_sem=ring_recv.at[which, head, part],
            device_id=((flow + 1) * ROW + core, tp),
            device_id_type=MESH,
        )

    def forward(indices):
        @pl.when(relays)
        def _():
            for index in indices:
                for flow in list(range(0, n_flow, 2)) + list(range(1, n_flow, 2)):
                    hop_copy(flow, index).wait_recv()
                    forward_copy(flow, index).start()

    def lat_copy(source, target, lane, device):
        return pltpu.make_async_remote_copy(
            src_ref=latall.at[source],
            dst_ref=latall.at[target],
            send_sem=lat_send.at[lane],
            recv_sem=lat_recv.at[lane],
            device_id=(device, tp),
            device_id_type=MESH,
        )

    lat_ring = functools.partial(lat_copy, 2, 0, 0, me + 2)
    lat_give = functools.partial(lat_copy, 2, 1, 1, partner)
    lat_cross = functools.partial(lat_copy, 2, 1, 1, me + 1)

    expected = n_tp + (1 + core) * has_next.astype(jnp.int32)
    if DETOUR:
        expected = expected + turns.astype(jnp.int32) + n_flow * relays.astype(jnp.int32)
    pl.semaphore_wait(barrier, expected)

    order = [(w, h, p) for h in range(kv - 1) for w in range(2) for p in (1, 0)]
    order += [(w, kv - 1, p) for p in (1, 0) for w in range(2)]

    straight = jnp.logical_and(has_next, jnp.logical_not(turns))

    def send(first, last):
        @pl.when(straight)
        def _():
            for item in order[first:last]:
                ring_copy(*item).start()

        @pl.when(turns)
        def _():
            for item in [item for item in order if item not in DETOUR][first:last]:
                ring_copy(*item).start()

    if DETOUR:
        @pl.when(turns)
        def _():
            for index in range(len(DETOUR)):
                hop_copy(lax.div(me, ROW), index).start()

    send(0, EARLY)

    @pl.when(core == 0)
    def _():
        for item in order:
            give_copy(*item).start()

    loads[0].wait()
    loads[1].wait()
    for load in loads[2:]:
        load.start()
    for head in range(kv):
        own_copy(0, head).start()
        own_copy(1, head).start()
    lat[tp] = jnp.dot(
        down_v[choice_ref[(me * tok) // SEG_LEN]], x_v[...], preferred_element_type=jnp.float32
    )

    def part_copy(step):
        return pltpu.make_async_remote_copy(
            src_ref=lat.at[tp],
            dst_ref=lat.at[tp],
            send_sem=part_send.at[step - 1],
            recv_sem=part_recv.at[step - 1],
            device_id=(me, tp_at(step)),
            device_id_type=MESH,
        )

    def part_arrival(step):
        slot = lat.at[tp_at(-step)]
        return pltpu.make_async_remote_copy(
            src_ref=slot,
            dst_ref=slot,
            send_sem=part_send.at[step - 1],
            recv_sem=part_recv.at[step - 1],
            device_id=(me, tp_at(step)),
            device_id_type=MESH,
        )

    for step in range(1, n_tp):
        part_copy(step).start()

    forward(range(0, min(1, len(DETOUR))))

    loads[2].wait()
    for source in range(3):
        segment = (jnp.maximum(me + source - 2, 0) * tok) // SEG_LEN
        upsel[source] = up_v[choice_ref[segment]]

    for step in range(1, n_tp):
        part_arrival(step).wait_recv()
    total = lat[0]
    for step in range(1, n_tp):
        total = total + lat[step]
    latall[2] = total.astype(jnp.bfloat16)

    @pl.when(core == 0)
    def _():
        lat_give().start()

    @pl.when(has_next)
    def _():
        @pl.when(core == 1)
        def _():
            lat_cross().start()

        lat_ring().start()

    send(EARLY, None)

    forward(range(1, len(DETOUR)))

    loads[3].wait()

    @pl.when(has_prev)
    def _():
        lat_ring().wait_recv()

    @pl.when(has_pair)
    def _():
        lat_give().wait_recv()

    row = lax.broadcasted_iota(jnp.int32, (half, half), 0)
    col = lax.broadcasted_iota(jnp.int32, (half, half), 1)
    later = col > row
    have = [has_prev, has_pair, None]

    def arrive(head, part):
        @pl.when(has_prev)
        def _():
            for which in range(2):
                ring_copy(which, head, part).wait_recv()

                @pl.when(core == 1)
                def _():
                    relay_copy(which, head, part).start()

    def arrive_pair(head, part):
        @pl.when(has_pair)
        def _():
            for which in range(2):
                give_copy(which, head, part).wait_recv()

    def fill_values(head, source, part, count):
        update = lax.dot_general(
            latall[source, :, pl.ds(part * half, count * half)], upsel[source, :, columns(head)],
            (((0,), (0,)), ((), ())), preferred_element_type=jnp.float32,
        )
        rows = pl.ds(source * tok + part * half, count * half)
        vf[rows, :] = (vraw[head, rows, :].astype(jnp.float32) + update).astype(jnp.bfloat16)

    def attend(head, block, member, runs, keep=False, resume=False):
        at = columns(2 * head + member)
        rows = q_v[pl.ds(block * half, half), at]
        scores, tops = [], {}
        for start, segments in runs:
            width = sum(segment[0] for segment in segments)
            s = lax.dot_general(
                rows, kall[head, pl.ds(start, width), :],
                (((1,), (1,)), ((), ())), preferred_element_type=jnp.float32,
            )
            cut = []
            first = 0
            for length, source, mask in segments:
                piece = s[:, first : first + length]
                if mask == "far":
                    piece = jnp.where(later, piece, NEG)
                if mask == "own":
                    piece = jnp.where(later, NEG, piece)
                cut.append(piece)
                tops.setdefault(source, []).append(piece)
                first += length
            scores.append(cut)
        top = None
        for source, pieces in tops.items():
            part = jnp.max(
                pieces[0] if len(pieces) == 1 else jnp.concatenate(pieces, axis=1),
                axis=1, keepdims=True,
            )
            if have[source] is not None:
                part = jnp.where(have[source], part, NEG)
            top = part if top is None else jnp.maximum(top, part)
        top = top * SCALE2
        if resume:
            old = m_s[block, member]
            top = jnp.maximum(top, old)
            fade = jnp.exp2(old - top)
        shift = {
            source: top if have[source] is None else jnp.where(have[source], top, BIG)
            for source in tops
        }
        norm, out = None, None
        for cut, (start, segments) in zip(scores, runs):
            expo = [
                jnp.exp2(piece * SCALE2 - shift[source])
                for piece, (_, source, _) in zip(cut, segments)
            ]
            expo = expo[0] if len(expo) == 1 else jnp.concatenate(expo, axis=1)
            part = jnp.sum(expo, axis=1, keepdims=True)
            norm = part if norm is None else norm + part
            part = jnp.dot(
                expo.astype(jnp.bfloat16), vf[pl.ds(start, expo.shape[1]), :],
                preferred_element_type=jnp.float32,
            )
            out = part if out is None else out + part
        if resume:
            norm = norm + fade * l_s[block, member]
            out = out + fade * acc_s[block, member]
        if keep:
            m_s[block, member] = top
            l_s[block, member] = norm
            acc_s[block, member] = out
        else:
            out_ref[pl.ds(block * half, half), at] = (out / norm).astype(jnp.bfloat16)

    def one_head(head, carry):
        own_copy(0, head).wait()
        own_copy(1, head).wait()
        for part in (1, 0):
            arrive(head, part)
        for part in (1, 0):
            arrive_pair(head, part)
        for source in range(3):
            fill_values(head, source, 0, 2)
        for member in range(2):
            attend(head, 0, member, [
                (0, [(half, 0, "far"), (half, 0, None), (tok, 1, None), (half, 2, "own")]),
            ])
            attend(head, 1, member, [
                (half, [(half, 0, "far"), (tok, 1, None), (half, 2, None), (half, 2, "own")]),
            ])
        return carry

    lax.fori_loop(0, kv - 1, one_head, 0)

    head = kv - 1
    own_copy(0, head).wait()
    own_copy(1, head).wait()
    fill_values(head, 2, 0, 2)
    arrive(head, 1)
    fill_values(head, 0, 1, 1)
    arrive_pair(head, 1)
    fill_values(head, 1, 1, 1)
    for member in range(2):
        attend(head, 0, member, [
            (half, [(half, 0, None)]),
            (tok + half, [(half, 1, None), (half, 2, "own")]),
        ], keep=True)
        attend(head, 1, member, [
            (half, [(half, 0, "far")]),
            (tok + half, [(half, 1, None), (half, 2, None), (half, 2, "own")]),
        ], keep=True)
    arrive(head, 0)
    fill_values(head, 0, 0, 1)
    arrive_pair(head, 0)
    fill_values(head, 1, 0, 1)
    for member in range(2):
        attend(head, 0, member, [
            (0, [(half, 0, "far")]),
            (tok, [(half, 1, None)]),
        ], resume=True)
        attend(head, 1, member, [
            (tok, [(half, 1, None)]),
        ], resume=True)

    for step in range(1, n_tp):
        part_copy(step).wait_send()

    @pl.when(has_next)
    def _():
        lat_ring().wait_send()
        for item in order:
            if item not in DETOUR:
                ring_copy(*item).wait_send()

    if DETOUR:
        @pl.when(straight)
        def _():
            for item in DETOUR:
                ring_copy(*item).wait_send()

        @pl.when(turns)
        def _():
            for index in range(len(DETOUR)):
                hop_copy(lax.div(me, ROW), index).wait_send()

        @pl.when(relays)
        def _():
            for index in range(len(DETOUR)):
                for flow in range(n_flow):
                    forward_copy(flow, index).wait_send()

    @pl.when(jnp.logical_or(core == 0, has_next))
    def _():
        lat_give().wait_send()

    @pl.when(jnp.logical_or(core == 0, has_prev))
    def _():
        for item in order:
            give_copy(*item).wait_send()


def on_device(
    n_seq, n_tp,
    normed_input, query, key, value, adapter_down_maps, adapter_up_maps, block_adapter_choice,
):
    tok, width = normed_input.shape
    kv = key.shape[1] // HEAD_WIDTH
    count, rank, columns = adapter_up_maps.shape
    n_flow = n_seq // ROW - 1
    n_hop = max(1, len(DETOUR))
    bf16, f32 = jnp.bfloat16, jnp.float32
    dma = pltpu.SemaphoreType.DMA
    hbm = pl.BlockSpec(memory_space=pl.ANY)
    return pl.pallas_call(
        functools.partial(kernel, n_seq, n_tp),
        out_shape=pltpu.VMEM(query.shape, bf16),
        in_specs=[pl.BlockSpec(memory_space=pltpu.SMEM)] + [hbm] * 6,
        out_specs=pl.BlockSpec(memory_space=pltpu.VMEM),
        scratch_shapes=[
            pltpu.VMEM((width, tok), bf16),
            pltpu.VMEM((count, rank, width), bf16),
            pltpu.VMEM((count, rank, columns), bf16),
            pltpu.VMEM(query.shape, bf16),
            pltpu.VMEM((kv, 3 * tok, HEAD_WIDTH), bf16),
            pltpu.VMEM((kv, 3 * tok, HEAD_WIDTH), bf16),
            pltpu.VMEM((3 * tok, HEAD_WIDTH), bf16),
            pltpu.VMEM((n_tp, rank, tok), f32),
            pltpu.VMEM((3, rank, tok), bf16),
            pltpu.VMEM((3, rank, columns), bf16),
            pltpu.VMEM((n_flow, n_hop, tok // 2, HEAD_WIDTH), bf16),
            pltpu.VMEM((2, 2, tok // 2, 1), f32),
            pltpu.VMEM((2, 2, tok // 2, 1), f32),
            pltpu.VMEM((2, 2, tok // 2, HEAD_WIDTH), f32),
            dma((4,)),
            dma((2, kv)),
            dma((2, kv, 2)), dma((2, kv, 2)), dma((2, kv, 2)), dma((2, kv, 2)),
            dma((n_tp - 1,)), dma((n_tp - 1,)), dma((2,)), dma((2,)),
            dma((n_hop,)), dma((n_flow, n_hop)), dma((n_flow, n_hop)),
        ],
        compiler_params=pltpu.CompilerParams(collective_id=0, has_side_effects=True),
    )(
        block_adapter_choice, normed_input.T, query, key, value,
        adapter_down_maps, adapter_up_maps,
    )


def solution(mesh):
    placed = (
        P("seq", "tp"),
        P("seq", "tp"),
        P("seq", "tp"),
        P("seq", "tp"),
        P(None, None, "tp"),
        P(None, None, "tp"),
        P(),
    )
    return jax.shard_map(
        functools.partial(on_device, mesh.shape["seq"], mesh.shape["tp"]),
        mesh=mesh, in_specs=placed, out_specs=P("seq", "tp"), check_vma=False,
    )
```

time: 42.2 us -> 36.8 us (0.87)
  the two profiles are of different devices: /device:TPU:1 before, /device:TPU:18 now
where the time goes in v2:
time: 36.8 us; the launch traced here: 36.7 us
  Pallas kernels  35.7 us (97%)
  local copies, waits for them, and re-layouts  0.97 us (3%)
    pallas_call x1, Pallas kernels, on_device(): pl.pallas_call(functools.partial(kernel, n_seq, n_tp), out_shape=pltpu.VM...  35.7 us
    unnamed x1, local copies, waits for them, and re-layouts  0.97 us

profile of v2, /device:TPU:18, one launch (start us, length us, event | category | flops | bytes accessed | tf_op | source)
XLA Modules:
  0.0 36.7 jit_solution(10386987651372267009)
XLA Ops:
  0.0 35.7 %shard_map.73 = bf16[512,1024]{1,0:T(8,128)(2,1)S(1)} custom-call(s32[16]{0:T(128)} %choice_ref.1, bf16[1344,512]{1,0:T(8,128)(2,1)} %bitcast.1, bf16[512,1024]{1,0:T(8,128)(2,1)} %q_ref.1, bf16[512,512]{1,0:T(8,128)(2,1)} %k_ref.1, bf16[512,512]{1,0:T(8,128)(2,1)} %v_ref.1, bf16[64,16,1344]{2,1,0:T(8,128)(2,1)} %down_ref.1, bf16[64,16,512]{2,1,0:T(8,128)(2,1)} %up_ref.1), custom_call_target="tpu_custom_call" | custom-call | tf_op jit(solution)/shard_map/pallas_call | solution.py:481
  35.7 1.0 %copy.9 = bf16[512,1024]{1,0:T(8,128)(2,1)} copy(bf16[512,1024]{1,0:T(8,128)(2,1)S(1)} %shard_map.73) | data formatting | bytes 2097152

commit v3 on v2

--- a/solution.py
+++ b/solution.py
@@ -11,7 +11,7 @@
 SEG_LEN = 2048
 MESH = pl.DeviceIdType.MESH
 EARLY = 6
-SCALE2 = 168.0 ** (-0.5) * 1.4426950408889634
+QUERY_SCALE = 168.0 ** (-0.5)
 NEG = -1e30
 BIG = 1e30
 ROW = 16
@@ -22,7 +22,7 @@
     n_seq, n_tp,
     choice_ref, x_ref, q_ref, k_ref, v_ref, down_ref, up_ref,
     out_ref,
-    x_v, down_v, up_v, q_v, kall, vraw, vf, lat, latall, upsel, hold, m_s, l_s, acc_s,
+    x_v, down_v, up_v, q_v, kall, vraw, vf, lat, latall, upsel, hold, m_s, acc_s,
     in_sem, kv_sem,
     ring_send, ring_recv, pair_send, pair_recv,
     part_send, part_recv, lat_send, lat_recv,
@@ -159,7 +159,7 @@
         @pl.when(relays)
         def _():
             for index in indices:
-                for flow in list(range(0, n_flow, 2)) + list(range(1, n_flow, 2)):
+                for flow in (1, 0, 2):
                     hop_copy(flow, index).wait_recv()
                     forward_copy(flow, index).start()
 
@@ -210,6 +210,8 @@
     def _():
         for item in order:
             give_copy(*item).start()
+
+    vf[:, HEAD_WIDTH:] = jnp.ones((3 * tok, HEAD_WIDTH), vf.dtype)
 
     loads[0].wait()
     loads[1].wait()
@@ -246,7 +248,7 @@
     for step in range(1, n_tp):
         part_copy(step).start()
 
-    forward(range(0, min(1, len(DETOUR))))
+    forward(range(len(DETOUR)))
 
     loads[2].wait()
     for source in range(3):
@@ -274,8 +276,6 @@
 
     send(EARLY, None)
 
-    forward(range(1, len(DETOUR)))
-
     loads[3].wait()
 
     @pl.when(has_prev)
@@ -313,71 +313,80 @@
             (((0,), (0,)), ((), ())), preferred_element_type=jnp.float32,
         )
         rows = pl.ds(source * tok + part * half, count * half)
-        vf[rows, :] = (vraw[head, rows, :].astype(jnp.float32) + update).astype(jnp.bfloat16)
-
-    def attend(head, block, member, runs, keep=False, resume=False):
-        at = columns(2 * head + member)
-        rows = q_v[pl.ds(block * half, half), at]
-        scores, tops = [], {}
-        for start, segments in runs:
-            width = sum(segment[0] for segment in segments)
-            s = lax.dot_general(
-                rows, kall[head, pl.ds(start, width), :],
-                (((1,), (1,)), ((), ())), preferred_element_type=jnp.float32,
-            )
-            cut = []
-            first = 0
-            for length, source, mask in segments:
-                piece = s[:, first : first + length]
-                if mask == "far":
-                    piece = jnp.where(later, piece, NEG)
-                if mask == "own":
-                    piece = jnp.where(later, NEG, piece)
-                cut.append(piece)
-                tops.setdefault(source, []).append(piece)
-                first += length
-            scores.append(cut)
-        top = None
-        for source, pieces in tops.items():
-            part = jnp.max(
-                pieces[0] if len(pieces) == 1 else jnp.concatenate(pieces, axis=1),
-                axis=1, keepdims=True,
-            )
-            if have[source] is not None:
-                part = jnp.where(have[source], part, NEG)
-            top = part if top is None else jnp.maximum(top, part)
-        top = top * SCALE2
-        if resume:
-            old = m_s[block, member]
-            top = jnp.maximum(top, old)
-            fade = jnp.exp2(old - top)
-        shift = {
-            source: top if have[source] is None else jnp.where(have[source], top, BIG)
-            for source in tops
-        }
-        norm, out = None, None
-        for cut, (start, segments) in zip(scores, runs):
-            expo = [
-                jnp.exp2(piece * SCALE2 - shift[source])
-                for piece, (_, source, _) in zip(cut, segments)
-            ]
-            expo = expo[0] if len(expo) == 1 else jnp.concatenate(expo, axis=1)
-            part = jnp.sum(expo, axis=1, keepdims=True)
-            norm = part if norm is None else norm + part
-            part = jnp.dot(
-                expo.astype(jnp.bfloat16), vf[pl.ds(start, expo.shape[1]), :],
-                preferred_element_type=jnp.float32,
-            )
-            out = part if out is None else out + part
-        if resume:
-            norm = norm + fade * l_s[block, member]
-            out = out + fade * acc_s[block, member]
-        if keep:
-            m_s[block, member] = top
-            l_s[block, member] = norm
-            acc_s[block, member] = out
-        else:
-            out_ref[pl.ds(block * half, half), at] = (out / norm).astype(jnp.bfloat16)
+        vf[rows, :HEAD_WIDTH] = (vraw[head, rows, :].astype(jnp.float32) + update).astype(jnp.bfloat16)
+
+    def attend(head, jobs, keep=False, resume=False):
+        scores = []
+        for block, member, runs in jobs:
+            rows = q_v[pl.ds(block * half, half), columns(2 * head + member)]
+            parts = []
+            for start, segments in runs:
+                width = sum(segment[0] for segment in segments)
+                s = lax.dot_general(
+                    rows, kall[head, pl.ds(start, width), :],
+                    (((1,), (1,)), ((), ())), preferred_element_type=jnp.float32,
+                )
+                cut = []
+                first = 0
+                for length, _, mask in segments:
+                    piece = s[:, first : first + length]
+                    if mask == "far":
+                        piece = jnp.where(later, piece, NEG)
+                    if mask == "own":
+                        piece = jnp.where(later, NEG, piece)
+                    cut.append(piece)
+                    first += length
+                parts.append(cut)
+            scores.append(parts)
+        tops, fades = [], []
+        for (block, member, runs), parts in zip(jobs, scores):
+            found = {}
+            for cut, (_, segments) in zip(parts, runs):
+                for piece, (_, source, _) in zip(cut, segments):
+                    found.setdefault(source, []).append(piece)
+            top = None
+            for source, pieces in found.items():
+                part = jnp.max(
+                    pieces[0] if len(pieces) == 1 else jnp.concatenate(pieces, axis=1),
+                    axis=1, keepdims=True,
+                )
+                if have[source] is not None:
+                    part = jnp.where(have[source], part, NEG)
+                top = part if top is None else jnp.maximum(top, part)
+            top = top * QUERY_SCALE
+            if resume:
+                old = m_s[block, member]
+                top = jnp.maximum(top, old)
+                fades.append(jnp.exp(old - top))
+            tops.append(top)
+        weights = []
+        for (block, member, runs), parts, top in zip(jobs, scores, tops):
+            shift = [jnp.where(known, top, BIG) if known is not None else top for known in have]
+            weights.append([
+                [
+                    jnp.exp(piece * QUERY_SCALE - shift[source]).astype(jnp.bfloat16)
+                    for piece, (_, source, _) in zip(cut, segments)
+                ]
+                for cut, (_, segments) in zip(parts, runs)
+            ])
+        for index, (block, member, runs) in enumerate(jobs):
+            out = None
+            for cut, (start, _) in zip(weights[index], runs):
+                expo = cut[0] if len(cut) == 1 else jnp.concatenate(cut, axis=1)
+                part = jnp.dot(
+                    expo, vf[pl.ds(start, expo.shape[1]), :], preferred_element_type=jnp.float32
+                )
+                out = part if out is None else out + part
+            if resume:
+                out = out + fades[index] * acc_s[block, member]
+            if keep:
+                m_s[block, member] = tops[index]
+                acc_s[block, member] = out
+            else:
+                out = out[:, :HEAD_WIDTH] / out[:, HEAD_WIDTH:]
+                out_ref[pl.ds(block * half, half), columns(2 * head + member)] = out.astype(
+                    jnp.bfloat16
+                )
 
     def one_head(head, carry):
         own_copy(0, head).wait()
@@ -388,13 +397,10 @@
             arrive_pair(head, part)
         for source in range(3):
             fill_values(head, source, 0, 2)
-        for member in range(2):
-            attend(head, 0, member, [
-                (0, [(half, 0, "far"), (half, 0, None), (tok, 1, None), (half, 2, "own")]),
-            ])
-            attend(head, 1, member, [
-                (half, [(half, 0, "far"), (tok, 1, None), (half, 2, None), (half, 2, "own")]),
-            ])
+        near = [(0, [(half, 0, "far"), (half, 0, None), (tok, 1, None), (half, 2, "own")])]
+        wide = [(half, [(half, 0, "far"), (tok, 1, None), (half, 2, None), (half, 2, "own")])]
+        attend(head, [(0, member, near) for member in range(2)])
+        attend(head, [(1, member, wide) for member in range(2)])
         return carry
 
     lax.fori_loop(0, kv - 1, one_head, 0)
@@ -407,27 +413,24 @@
     fill_values(head, 0, 1, 1)
     arrive_pair(head, 1)
     fill_values(head, 1, 1, 1)
-    for member in range(2):
-        attend(head, 0, member, [
-            (half, [(half, 0, None)]),
-            (tok + half, [(half, 1, None), (half, 2, "own")]),
-        ], keep=True)
-        attend(head, 1, member, [
-            (half, [(half, 0, "far")]),
-            (tok + half, [(half, 1, None), (half, 2, None), (half, 2, "own")]),
-        ], keep=True)
+    near = [(half, [(half, 0, None)]), (tok + half, [(half, 1, None), (half, 2, "own")])]
+    wide = [
+        (half, [(half, 0, "far")]),
+        (tok + half, [(half, 1, None), (half, 2, None), (half, 2, "own")]),
+    ]
+    attend(head, [(0, member, near) for member in range(2)], keep=True)
+    attend(head, [(1, member, wide) for member in range(2)], keep=True)
     arrive(head, 0)
     fill_values(head, 0, 0, 1)
     arrive_pair(head, 0)
     fill_values(head, 1, 0, 1)
-    for member in range(2):
-        attend(head, 0, member, [
-            (0, [(half, 0, "far")]),
-            (tok, [(half, 1, None)]),
-        ], resume=True)
-        attend(head, 1, member, [
-            (tok, [(half, 1, None)]),
-        ], resume=True)
+    near = [(0, [(half, 0, "far")]), (tok, [(half, 1, None)])]
+    wide = [(tok, [(half, 1, None)])]
+    attend(
+        head,
+        [(0, member, near) for member in range(2)] + [(1, member, wide) for member in range(2)],
+        resume=True,
+    )
 
     for step in range(1, n_tp):
         part_copy(step).wait_send()
@@ -490,14 +493,13 @@
             pltpu.VMEM(query.shape, bf16),
             pltpu.VMEM((kv, 3 * tok, HEAD_WIDTH), bf16),
             pltpu.VMEM((kv, 3 * tok, HEAD_WIDTH), bf16),
-            pltpu.VMEM((3 * tok, HEAD_WIDTH), bf16),
+            pltpu.VMEM((3 * tok, 2 * HEAD_WIDTH), bf16),
             pltpu.VMEM((n_tp, rank, tok), f32),
             pltpu.VMEM((3, rank, tok), bf16),
             pltpu.VMEM((3, rank, columns), bf16),
             pltpu.VMEM((n_flow, n_hop, tok // 2, HEAD_WIDTH), bf16),
             pltpu.VMEM((2, 2, tok // 2, 1), f32),
-            pltpu.VMEM((2, 2, tok // 2, 1), f32),
-            pltpu.VMEM((2, 2, tok // 2, HEAD_WIDTH), f32),
+            pltpu.VMEM((2, 2, tok // 2, 2 * HEAD_WIDTH), f32),
             dma((4,)),
             dma((2, kv)),
             dma((2, kv, 2)), dma((2, kv, 2)), dma((2, kv, 2)), dma((2, kv, 2)),

time: 36.8 us -> 34.5 us (0.938)
  the two profiles are of different devices: /device:TPU:18 before, /device:TPU:24 now
where the time goes in v3:
time: 34.5 us; the launch traced here: 34.4 us
  Pallas kernels  33.4 us (97%)
  local copies, waits for them, and re-layouts  0.97 us (3%)
    pallas_call x1, Pallas kernels, on_device(): pl.pallas_call(functools.partial(kernel, n_seq, n_tp), out_shape=pltpu.VM...  33.4 us
    unnamed x1, local copies, waits for them, and re-layouts  0.97 us

profile of v3, /device:TPU:24, one launch (start us, length us, event | category | flops | bytes accessed | tf_op | source)
XLA Modules:
  0.0 34.4 jit_solution(2375348488946770171)
XLA Ops:
  0.0 33.4 %shard_map.73 = bf16[512,1024]{1,0:T(8,128)(2,1)S(1)} custom-call(s32[16]{0:T(128)} %choice_ref.1, bf16[1344,512]{1,0:T(8,128)(2,1)} %bitcast.1, bf16[512,1024]{1,0:T(8,128)(2,1)} %q_ref.1, bf16[512,512]{1,0:T(8,128)(2,1)} %k_ref.1, bf16[512,512]{1,0:T(8,128)(2,1)} %v_ref.1, bf16[64,16,1344]{2,1,0:T(8,128)(2,1)} %down_ref.1, bf16[64,16,512]{2,1,0:T(8,128)(2,1)} %up_ref.1), custom_call_target="tpu_custom_call" | custom-call | tf_op jit(solution)/shard_map/pallas_call | solution.py:484
  33.4 1.0 %copy.9 = bf16[512,1024]{1,0:T(8,128)(2,1)} copy(bf16[512,1024]{1,0:T(8,128)(2,1)S(1)} %shard_map.73) | data formatting | bytes 2097152

commit v4 on v3

--- a/solution.py
+++ b/solution.py
@@ -307,11 +307,15 @@
             for which in range(2):
                 give_copy(which, head, part).wait_recv()
 
-    def fill_values(head, source, part, count):
-        update = lax.dot_general(
+    def update_of(head, source, part, count):
+        return lax.dot_general(
             latall[source, :, pl.ds(part * half, count * half)], upsel[source, :, columns(head)],
             (((0,), (0,)), ((), ())), preferred_element_type=jnp.float32,
         )
+
+    def fill_values(head, source, part, count, update=None):
+        if update is None:
+            update = update_of(head, source, part, count)
         rows = pl.ds(source * tok + part * half, count * half)
         vf[rows, :HEAD_WIDTH] = (vraw[head, rows, :].astype(jnp.float32) + update).astype(jnp.bfloat16)
 
@@ -409,10 +413,13 @@
     own_copy(0, head).wait()
     own_copy(1, head).wait()
     fill_values(head, 2, 0, 2)
+    updates = {
+        (source, part): update_of(head, source, part, 1) for source in range(2) for part in range(2)
+    }
     arrive(head, 1)
-    fill_values(head, 0, 1, 1)
+    fill_values(head, 0, 1, 1, updates[0, 1])
     arrive_pair(head, 1)
-    fill_values(head, 1, 1, 1)
+    fill_values(head, 1, 1, 1, updates[1, 1])
     near = [(half, [(half, 0, None)]), (tok + half, [(half, 1, None), (half, 2, "own")])]
     wide = [
         (half, [(half, 0, "far")]),
@@ -421,9 +428,9 @@
     attend(head, [(0, member, near) for member in range(2)], keep=True)
     attend(head, [(1, member, wide) for member in range(2)], keep=True)
     arrive(head, 0)
-    fill_values(head, 0, 0, 1)
+    fill_values(head, 0, 0, 1, updates[0, 0])
     arrive_pair(head, 0)
-    fill_values(head, 1, 0, 1)
+    fill_values(head, 1, 0, 1, updates[1, 0])
     near = [(0, [(half, 0, "far")]), (tok, [(half, 1, None)])]
     wide = [(tok, [(half, 1, None)])]
     attend(

time: 34.5 us -> 34.1 us (0.988)
  Pallas kernels: 33.4 us -> 33 us
    pallas_call x1, Pallas kernels: 33.4 us -> 33 us  [on_device(): pl.pallas_call(functools.partial(kernel, n_seq, n_tp), out_shape=pltpu.VM...]
where the time goes in v4:
time: 34.1 us; the launch traced here: 34 us
  Pallas kernels  33 us (97%)
  local copies, waits for them, and re-layouts  0.97 us (3%)
    pallas_call x1, Pallas kernels, on_device(): pl.pallas_call(functools.partial(kernel, n_seq, n_tp), out_shape=pltpu.VM...  33 us
    unnamed x1, local copies, waits for them, and re-layouts  0.97 us

profile of v4, /device:TPU:24, one launch (start us, length us, event | category | flops | bytes accessed | tf_op | source)
XLA Modules:
  0.0 34.0 jit_solution(3190851262836125415)
XLA Ops:
  0.0 33.0 %shard_map.73 = bf16[512,1024]{1,0:T(8,128)(2,1)S(1)} custom-call(s32[16]{0:T(128)} %choice_ref.1, bf16[1344,512]{1,0:T(8,128)(2,1)} %bitcast.1, bf16[512,1024]{1,0:T(8,128)(2,1)} %q_ref.1, bf16[512,512]{1,0:T(8,128)(2,1)} %k_ref.1, bf16[512,512]{1,0:T(8,128)(2,1)} %v_ref.1, bf16[64,16,1344]{2,1,0:T(8,128)(2,1)} %down_ref.1, bf16[64,16,512]{2,1,0:T(8,128)(2,1)} %up_ref.1), custom_call_target="tpu_custom_call" | custom-call | tf_op jit(solution)/shard_map/pallas_call | solution.py:491
  33.0 1.0 %copy.9 = bf16[512,1024]{1,0:T(8,128)(2,1)} copy(bf16[512,1024]{1,0:T(8,128)(2,1)S(1)} %shard_map.73) | data formatting | bytes 2097152
